TPU v7x, 256 devices: a whole 4x4x8 slice. The times are simulated.
256 devices in a mesh: filt: 2 (over core), row: 4 (over x), col: 32 (over z, y).
Axes of the slice: x: 4, y: 4, z: 8, core: 2. Of those that a mesh axis runs over, the one named last changes fastest.
Arguments:
- particles: bfloat16 [24576, 256], P(('filt', 'row', 'col')), parts along dimension 0, may hold values from -6 to 6
- cotangent: bfloat16 [24576, 256], P(('filt', 'row', 'col')), parts along dimension 0, may hold values from -3 to 3
- row_potential: bfloat16 [24576], P(('filt', 'row', 'col')), parts along dimension 0, may hold values from -0.099609375 to 0.099609375
- col_potential: bfloat16 [24576], P(('filt', 'row', 'col')), parts along dimension 0, may hold values from -0.099609375 to 0.099609375
- weights: bfloat16 [24576], P(('filt', 'row', 'col')), parts along dimension 0, may hold values from 0.5 to 18
Outputs:
- grad_particles: bfloat16 [24576, 256], P(('filt', 'row', 'col')), parts along dimension 0
- grad_weights: float32 [24576], P(('filt', 'row', 'col')), parts along dimension 0
There are 2 independent parts, one for each index of `filt`. A program takes and returns all parts, laid end to end along the dimension named above; each array names one. Nothing has to cross between parts.
All inputs are finite; a program needn't handle non-finite values.
Results may differ from a plain program's by a relative error of at most 0.02.
Values may be sent and summed in bfloat16 or wider, within the bound.
No kernel may reach another device: no remote copies, remote signals or barrier semaphores. Data moves between devices by JAX's collectives and lax.ppermute only.
A program may use at most 64 MiB of HBM per device.

v0:
```python
import jax
import jax.numpy as jnp
from jax import lax
from jax.sharding import PartitionSpec as P

ITERS = 4
EPS = 0.09


def local(particles, cotangent, row_potential, col_potential, weights):
    row_parts, row_fpot, row_wts = (
        lax.all_gather(particles, "col", axis=0, tiled=True),
        lax.all_gather(row_potential, "col", axis=0, tiled=True),
        lax.all_gather(weights, "col", axis=0, tiled=True),
    )
    col_parts, col_grads, col_gpot = (
        lax.all_gather(particles, "row", axis=0, tiled=True),
        lax.all_gather(cotangent, "row", axis=0, tiled=True),
        lax.all_gather(col_potential, "row", axis=0, tiled=True),
    )
    own = particles.shape[0]
    width = particles.shape[1]
    rows = row_parts.shape[0]
    cols = col_parts.shape[0]
    blk = 512
    count = rows // blk
    row_float = row_parts.astype(jnp.float32)
    row_sq = jnp.sum(row_float * row_float, axis=1)
    col_float = col_parts.astype(jnp.float32)
    col_sq = jnp.sum(col_float * col_float, axis=1)
    fpot = row_fpot.astype(jnp.float32)
    gpot = col_gpot.astype(jnp.float32)
    stacked = jnp.concatenate([col_parts, col_grads], axis=0)
    items = (
        row_parts.reshape(count, blk, width),
        fpot.reshape(count, blk),
        row_sq.reshape(count, blk),
    )

    def plan_from(cross, pot_blk, sq_blk):
        cost = (sq_blk[:, None] + col_sq[None, :] - 2.0 * cross) / (2.0 * width)
        return jnp.exp((pot_blk[:, None] + gpot[None, :] - cost) / EPS)

    def plan_only(part_blk, pot_blk, sq_blk):
        cross = jnp.einsum("rd,cd->rc", part_blk, col_parts, preferred_element_type=jnp.float32)
        return plan_from(cross, pot_blk, sq_blk)

    def first(carry, item):
        part_blk, pot_blk, sq_blk = item
        both = jnp.einsum("rd,cd->rc", part_blk, stacked, preferred_element_type=jnp.float32)
        plan = plan_from(both[:, :cols], pot_blk, sq_blk)
        weighted = plan * both[:, cols:]
        return (
            (carry[0] + jnp.sum(plan, axis=0), carry[1] + jnp.sum(weighted, axis=0)),
            (jnp.sum(plan, axis=1), jnp.sum(weighted, axis=1)),
        )

    zeros_c = jnp.zeros((cols,), jnp.float32)
    (colmass_part, colph_part), (rowmass_part, rowph_part) = lax.scan(
        first, (zeros_c, zeros_c), items
    )
    rowmass, rowph = lax.psum((rowmass_part.reshape(rows), rowph_part.reshape(rows)), "col")
    colmass, colph = lax.psum((colmass_part, colph_part), "row")
    psi = zeros_c
    phi = jnp.zeros((rows,), jnp.float32)
    for step in range(ITERS):

        def apply_rows(carry, item):
            plan = plan_only(item[0], item[1], item[2])
            return (carry, jnp.dot(plan, psi, precision=lax.Precision.HIGHEST))

        unused, row_apply = lax.scan(apply_rows, jnp.zeros((), jnp.float32), items)
        row_total = lax.psum(row_apply.reshape(rows), "col")
        phi = -(rowph + row_total) / rowmass

        def apply_cols(acc, item):
            plan = plan_only(item[0], item[1], item[2])
            return (acc + jnp.dot(item[3], plan, precision=lax.Precision.HIGHEST), None)

        col_apply, unused_out = lax.scan(apply_cols, zeros_c, items + (phi.reshape(count, blk),))
        col_total = lax.psum(col_apply, "row")
        psi = -(colph + col_total) / colmass

    def last(acc, item):
        part_blk, pot_blk, sq_blk, phi_blk = item
        both = jnp.einsum("rd,cd->rc", part_blk, stacked, preferred_element_type=jnp.float32)
        plan = plan_from(both[:, :cols], pot_blk, sq_blk)
        mixed = plan * (both[:, cols:] + phi_blk[:, None] + psi[None, :])
        qrow = jnp.sum(mixed, axis=1)
        plan_bf = plan.astype(jnp.bfloat16)
        mixed_bf = mixed.astype(jnp.bfloat16)
        rowterm = jnp.dot(plan_bf, col_grads, preferred_element_type=jnp.float32)
        rowterm = rowterm + (
            jnp.dot(mixed_bf, col_parts, preferred_element_type=jnp.float32)
            - qrow[:, None] * part_blk.astype(jnp.float32)
        ) / (width * EPS)
        return (
            acc + jnp.einsum("rc,rd->cd", mixed_bf, part_blk, preferred_element_type=jnp.float32),
            rowterm,
        )

    col_acc, row_terms = lax.scan(
        last, jnp.zeros((cols, width), jnp.float32), items + (phi.reshape(count, blk),)
    )
    row_terms = row_terms.reshape(rows, width)
    start = lax.axis_index("col") * own
    summed = lax.psum(row_terms.astype(jnp.bfloat16), "col").astype(jnp.float32)
    row_own = lax.dynamic_slice_in_dim(summed, start, own, 0)
    col_own = lax.psum_scatter(
        col_acc.astype(jnp.bfloat16), "row", scatter_dimension=0, tiled=True
    ).astype(jnp.float32)
    grad_particles = (row_own + col_own / (width * EPS)).astype(jnp.bfloat16)
    phi_own = lax.dynamic_slice_in_dim(phi, start, own, 0)
    own_wts = weights.astype(jnp.float32)
    total, wphi = lax.psum((jnp.sum(own_wts), jnp.sum(own_wts * phi_own)), ("row", "col"))
    count_all = rows * lax.axis_size("row")
    grad_weights = -(count_all / total) * (phi_own - wphi / total)
    return (grad_particles, grad_weights)


def solution(mesh):
    return jax.shard_map(
        local,
        mesh=mesh,
        in_specs=(
            P(("filt", "row", "col"), None),
            P(("filt", "row", "col"), None),
            P(("filt", "row", "col")),
            P(("filt", "row", "col")),
            P(("filt", "row", "col")),
        ),
        out_specs=(P(("filt", "row", "col"), None), P(("filt", "row", "col"))),
        check_vma=False,
    )
```

profile of v0, /device:TPU:8, one launch (start us, length us, event | category | flops | bytes accessed | tf_op | source)
XLA Modules:
  0.0 1151.9 jit_solution(2241112115767740689)
XLA Ops:
  8.0 1.3 dynamic-slice
  9.9 0.9 dynamic-update-slice
  10.7 75.0 %all-reduce = bf16[3072]{0:T(1024)(128)(2,1)S(1)} all-reduce(bf16[3072]{0:T(1024)(128)(2,1)S(1)} %dynamic-update-slice), channel_id=1, replica_groups=mesh['filt'=2,'row'=4,'col'=32] {'col'}, use_global_device_ids=true, to_apply=%add | all-reduce | flops 3072 | bytes 12288
  85.8 1.3 dynamic-slice.1
  87.6 0.9 dynamic-update-slice.1
  88.5 10.5 all-reduce.1
  99.0 12.3 %all_gather.18 = bf16[384,256]{1,0:T(8,128)(2,1)S(1)} all-gather(bf16[96,256]{1,0:T(8,128)(2,1)} %param.25), channel_id=1, replica_groups=mesh['filt'=2,'row'=4,'col'=32] {'row'}, dimensions={0}, use_global_device_ids=true | all-gather | bytes 245760 | tf_op jit(solution)/shard_map/all_gather | solution.py:17
  111.3 12.3 %all_gather.19 = bf16[384,256]{1,0:T(8,128)(2,1)S(1)} all-gather(bf16[96,256]{1,0:T(8,128)(2,1)} %param.26), channel_id=1, replica_groups=mesh['filt'=2,'row'=4,'col'=32] {'row'}, dimensions={0}, use_global_device_ids=true | all-gather | bytes 245760 | tf_op jit(solution)/shard_map/all_gather | solution.py:18
  123.9 2.0 multiply_reduce_fusion
  125.9 7.0 while.118
  132.9 7.5 while.117
  133.4 0.8 fusion.226
  134.6 0.8 fusion.226
  135.9 0.8 fusion.226
  137.1 0.8 fusion.226
  138.4 0.8 fusion.226
  139.6 0.8 fusion.226
  140.5 139.2 %all-reduce.3 = (f32[3072]{0:T(1024)S(1)}, f32[3072]{0:T(1024)S(1)}, f32[3072]{0:T(1024)S(1)}) all-reduce(f32[3072]{0:T(1024)S(1)} %reshape.119, f32[3072]{0:T(1024)S(1)} %reshape.117, f32[3072]{0:T(1024)S(1)} %reshape.118), channel_id=1, replica_groups=mesh['filt'=2,'row'=4,'col'=32] {'col'}, use_global_device_ids=true, to_apply=%region_13.14 | all-reduce | flops 9216 | bytes 73728 | tf_op jit(solution)/shard_map/psum | solution.py:62
  279.7 5.8 while.119
  285.5 7.9 all-reduce.4
  294.0 7.5 while.124
  300.6 0.8 fusion.268
  301.5 137.7 %psum.111 = f32[3072]{0:T(1024)S(1)} all-reduce(f32[3072]{0:T(1024)S(1)} %reshape.121), channel_id=1, replica_groups=mesh['filt'=2,'row'=4,'col'=32] {'col'}, use_global_device_ids=true, to_apply=%region_20.21 | all-reduce | flops 3072 | bytes 24576 | tf_op jit(solution)/shard_map/psum | solution.py:73
  439.2 5.8 while.120
  445.0 9.7 psum.112
  455.3 7.5 while.125
  462.8 137.7 %psum.113 = f32[3072]{0:T(1024)S(1)} all-reduce(f32[3072]{0:T(1024)S(1)} %reshape.123), channel_id=1, replica_groups=mesh['filt'=2,'row'=4,'col'=32] {'col'}, use_global_device_ids=true, to_apply=%region_26.27 | all-reduce | flops 3072 | bytes 24576 | tf_op jit(solution)/shard_map/psum | solution.py:73
  600.5 5.8 while.121
  606.3 7.7 psum.114
  614.7 7.5 while.126
  615.1 0.8 fusion.280
  616.3 0.8 fusion.280
  617.6 0.8 fusion.280
  618.8 0.8 fusion.280
  620.1 0.8 fusion.280
  621.3 0.8 fusion.280
  622.2 138.0 %psum.115 = f32[3072]{0:T(1024)S(1)} all-reduce(f32[3072]{0:T(1024)S(1)} %reshape.125), channel_id=1, replica_groups=mesh['filt'=2,'row'=4,'col'=32] {'col'}, use_global_device_ids=true, to_apply=%region_32.33 | all-reduce | flops 3072 | bytes 24576 | tf_op jit(solution)/shard_map/psum | solution.py:73
  760.2 5.8 while.122
  765.9 9.7 psum.116
  775.7 16.9 %while.123 = (s32[]{:T(128)}, f32[384,256]{1,0:T(8,128)S(1)}, bf16[6,512,256]{2,1,0:T(8,128)(2,1)}, f32[6,512]{1,0:T(8,128)S(1)}, f32[384]{0:T(512)S(1)}, /*inde...) while((s32[]{:T(128)}, f32[384,256]{1,0:T(8,128)S(1)}, ...), condition=%wide.region_38.39_spmd.clone, body=%wide.region_36.38_spmd.clone.sunk | while | flops 508100096 | bytes 9079975 | solution.py:102
  777.1 1.0 fusion.262
  779.9 1.0 fusion.262
  782.7 1.0 fusion.262
  785.5 1.0 fusion.262
  788.4 1.0 fusion.262
  791.2 1.0 fusion.262
  794.8 346.5 %all-reduce.2 = (f32[]{:T(128)}, f32[]{:T(128)}) all-reduce(f32[]{:T(128)} %get-tuple-element.718, f32[]{:T(128)} %get-tuple-element.717), channel_id=1, replica_groups=mesh['filt'=2,'row'=4,'col'=32] {'row','col'}, use_global_device_ids=true, to_apply=%region_44.45 | all-reduce | flops 2 | bytes 16 | tf_op jit(solution)/shard_map/psum | solution.py:115
  1143.9 1.5 add_convert_fusion
  (322 shorter events, 64.2 us)
Async XLA Ops:
  7.2 116.7 %all-gather.2.cloned.1.call-start = ((), (), s32[]{:S(2)}) async-start(), calls=%async_computation.1 | async-start | bytes 1622016 | tf_op jit(solution)/shard_map/all_gather | solution.py:12
  7.9 1136.0 %reduce-scatter.2.cloned.1.call-start = ((), (), s32[]{:S(2)}) async-start(), calls=%async_computation.3 | async-start | bytes 245760 | tf_op jit(solution)/shard_map/reduce_scatter | solution.py:109
  123.8 2.1 copy-start
  293.4 0.6 copy-start.2
  454.7 0.6 copy-start.3
  614.1 0.6 copy-start.1
  792.6 1.5 copy-start.4
  793.4 350.6 %all-reduce.7.cloned.1.call-start = ((), (), s32[]{:S(2)}) async-start(), calls=%async_computation.2 | async-start | bytes 3145728 | tf_op jit(solution)/shard_map/psum | solution.py:107
Sparse Core Ops, SparseCore 0:
  10.6 78.8 all-gather.1
  793.5 18.2 reduce-scatter.1
  815.6 149.9 all-reduce.6
where the time goes:
time: 1150 us
  blocking collectives  1040 us (90%)
  matrix products  65.2 us (6%)
  between operations  17.3 us (2%)
  other arithmetic  12.4 us (1%)
    psum x3, blocking collectives, local(): row_total = lax.psum(row_apply.reshape(rows), 'col')  413 us
    psum x1, blocking collectives, local(): lax.psum((jnp.sum(own_wts), jnp.sum(own_wts * phi_own)), ('row', 'col'))  347 us
    psum x1, blocking collectives, local(): lax.psum((rowmass_part.reshape(rows), rowph_part.reshape(rows)), 'col')  139 us
    unnamed x2, blocking collectives  85.5 us
    psum x3, blocking collectives, local(): col_total = lax.psum(col_apply, 'row')  27.2 us
  transfers between devices with their start and end apart: 3, of which 0 were waited for; matrix products, arithmetic and copies ran while one was open for 0% of the time, Pallas kernels for 0%

commit v1 on v0

--- a/solution.py
+++ b/solution.py
@@ -70,7 +70,12 @@
             return (carry, jnp.dot(plan, psi, precision=lax.Precision.HIGHEST))
 
         unused, row_apply = lax.scan(apply_rows, jnp.zeros((), jnp.float32), items)
-        row_total = lax.psum(row_apply.reshape(rows), "col")
+
+        def matrix_carry(local_block):
+            arr_now = jax.lax.all_gather(local_block, "col")
+            return jnp.sum(arr_now, axis=0)
+
+        row_total = matrix_carry(row_apply.reshape(rows))
         phi = -(rowph + row_total) / rowmass
 
         def apply_cols(acc, item):

time: 1150 us -> 931 us (0.81)
  blocking collectives: 1040 us -> 822 us
    psum x3 -> x0, blocking collectives: 413 us -> none  [local(): row_total = lax.psum(row_apply.reshape(rows), 'col')]
    all_gather x0 -> x4, blocking collectives: none -> 198 us  [matrix_carry(): arr_now = jax.lax.all_gather(local_block, 'col')]
  transfers between devices with their start and end apart: 3 -> 3, of which waited for: 0 -> 0; matrix products, arithmetic and copies ran while one was open for 0% -> 1% of each run, Pallas kernels for 0% -> 0%
where the time goes in v1:
time: 931 us; the launch traced here: 930 us
  blocking collectives  822 us (88%)
  matrix products  65.2 us (7%)
  between operations  17.4 us (2%)
  other arithmetic  13.3 us (1%)
    psum x1, blocking collectives, local(): lax.psum((jnp.sum(own_wts), jnp.sum(own_wts * phi_own)), ('row', 'col'))  343 us
    all_gather x4, blocking collectives, matrix_carry(): arr_now = jax.lax.all_gather(local_block, 'col')  198 us
    psum x1, blocking collectives, local(): lax.psum((rowmass_part.reshape(rows), rowph_part.reshape(rows)), 'col')  135 us
    unnamed x2, blocking collectives  85.5 us
    psum x3, blocking collectives, local(): col_total = lax.psum(col_apply, 'row')  27.5 us
    dot_general x48, matrix products, plan_only(): jnp.einsum('rd,cd->rc', part_blk, col_parts, preferred_element_type=jnp.f...  19.1 us
  transfers between devices with their start and end apart: 3, of which 0 were waited for; matrix products, arithmetic and copies ran while one was open for 1% of the time, Pallas kernels for 0%

profile of v1, /device:TPU:8, one launch (start us, length us, event | category | flops | bytes accessed | tf_op | source)
XLA Modules:
  0.0 930.5 jit_solution(11123894725908066340)
XLA Ops:
  8.0 1.3 dynamic-slice
  9.9 0.9 dynamic-update-slice
  10.7 75.0 %all-reduce = bf16[3072]{0:T(1024)(128)(2,1)S(1)} all-reduce(bf16[3072]{0:T(1024)(128)(2,1)S(1)} %dynamic-update-slice), channel_id=1, replica_groups=mesh['filt'=2,'row'=4,'col'=32] {'col'}, use_global_device_ids=true, to_apply=%add | all-reduce | flops 3072 | bytes 12288
  85.8 1.3 dynamic-slice.1
  87.6 0.9 dynamic-update-slice.1
  88.5 10.5 %all-reduce.1 = bf16[384]{0:T(512)(128)(2,1)S(1)} all-reduce(bf16[384]{0:T(512)(128)(2,1)S(1)} %dynamic-update-slice.1), channel_id=1, replica_groups=mesh['filt'=2,'row'=4,'col'=32] {'row'}, use_global_device_ids=true, to_apply=%add.1 | all-reduce | flops 384 | bytes 1536
  99.0 12.3 %all_gather.30 = bf16[384,256]{1,0:T(8,128)(2,1)S(1)} all-gather(bf16[96,256]{1,0:T(8,128)(2,1)} %param.25), channel_id=1, replica_groups=mesh['filt'=2,'row'=4,'col'=32] {'row'}, dimensions={0}, use_global_device_ids=true | all-gather | bytes 245760 | tf_op jit(solution)/shard_map/all_gather | solution.py:17
  111.3 12.3 %all_gather.31 = bf16[384,256]{1,0:T(8,128)(2,1)S(1)} all-gather(bf16[96,256]{1,0:T(8,128)(2,1)} %param.26), channel_id=1, replica_groups=mesh['filt'=2,'row'=4,'col'=32] {'row'}, dimensions={0}, use_global_device_ids=true | all-gather | bytes 245760 | tf_op jit(solution)/shard_map/all_gather | solution.py:18
  123.9 2.0 multiply_reduce_fusion
  125.9 7.0 while.118
  132.9 7.5 while.117
  133.4 0.8 fusion.226
  134.6 0.8 fusion.226
  135.9 0.8 fusion.226
  137.1 0.8 fusion.226
  138.4 0.8 fusion.226
  139.6 0.8 fusion.226
  140.5 51.0 %all-gather = f32[32,1,3072]{2,1,0:T(1,128)S(1)} all-gather(f32[1,1,3072]{2,1,0:T(1,128)S(1)} %reshape.119), channel_id=1, replica_groups=mesh['filt'=2,'row'=4,'col'=32] {'col'}, dimensions={0}, use_global_device_ids=true | all-gather | bytes 405504 | tf_op jit(solution)/shard_map/all_gather | solution.py:75
  191.5 134.8 %all-reduce.3 = (f32[3072]{0:T(1024)S(1)}, f32[3072]{0:T(1024)S(1)}) all-reduce(f32[3072]{0:T(1024)S(1)} %reshape.106, f32[3072]{0:T(1024)S(1)} %reshape.105), channel_id=1, replica_groups=mesh['filt'=2,'row'=4,'col'=32] {'col'}, use_global_device_ids=true, to_apply=%region_13.14 | all-reduce | flops 6144 | bytes 49152 | tf_op jit(solution)/shard_map/psum | solution.py:62
  326.6 5.8 while.119
  332.4 8.0 all-reduce.4
  340.9 7.5 while.124
  348.4 51.7 %all-gather.1 = f32[32,1,3072]{2,1,0:T(1,128)S(1)} all-gather(f32[1,1,3072]{2,1,0:T(1,128)S(1)} %reshape.121), channel_id=1, replica_groups=mesh['filt'=2,'row'=4,'col'=32] {'col'}, dimensions={0}, use_global_device_ids=true | all-gather | bytes 405504 | tf_op jit(solution)/shard_map/all_gather | solution.py:75
  400.4 5.8 while.120
  406.2 9.8 %psum.82 = f32[384]{0:T(512)S(1)} all-reduce(f32[384]{0:T(512)S(1)} %get-tuple-element.508), channel_id=1, replica_groups=mesh['filt'=2,'row'=4,'col'=32] {'row'}, use_global_device_ids=true, to_apply=%region_23.24 | all-reduce | flops 384 | bytes 3072 | tf_op jit(solution)/shard_map/psum | solution.py:86
  416.6 7.5 while.125
  424.1 46.2 %all-gather.2 = f32[32,1,3072]{2,1,0:T(1,128)S(1)} all-gather(f32[1,1,3072]{2,1,0:T(1,128)S(1)} %reshape.123), channel_id=1, replica_groups=mesh['filt'=2,'row'=4,'col'=32] {'col'}, dimensions={0}, use_global_device_ids=true | all-gather | bytes 405504 | tf_op jit(solution)/shard_map/all_gather | solution.py:75
  470.6 5.8 while.121
  476.3 8.0 psum.83
  484.9 7.5 while.126
  485.3 0.8 fusion.280
  486.6 0.8 fusion.280
  487.8 0.8 fusion.280
  489.1 0.8 fusion.280
  490.3 0.8 fusion.280
  491.6 0.8 fusion.280
  492.4 49.4 %all-gather.3 = f32[32,1,3072]{2,1,0:T(1,128)S(1)} all-gather(f32[1,1,3072]{2,1,0:T(1,128)S(1)} %reshape.125), channel_id=1, replica_groups=mesh['filt'=2,'row'=4,'col'=32] {'col'}, dimensions={0}, use_global_device_ids=true | all-gather | bytes 405504 | tf_op jit(solution)/shard_map/all_gather | solution.py:75
  542.2 5.8 while.122
  548.0 9.7 %psum.84 = f32[384]{0:T(512)S(1)} all-reduce(f32[384]{0:T(512)S(1)} %get-tuple-element.512), channel_id=1, replica_groups=mesh['filt'=2,'row'=4,'col'=32] {'row'}, use_global_device_ids=true, to_apply=%region_35.36 | all-reduce | flops 384 | bytes 3072 | tf_op jit(solution)/shard_map/psum | solution.py:86
  557.7 16.9 %while.123 = (s32[]{:T(128)}, f32[384,256]{1,0:T(8,128)S(1)}, bf16[6,512,256]{2,1,0:T(8,128)(2,1)}, f32[6,512]{1,0:T(8,128)S(1)}, f32[384]{0:T(512)S(1)}, /*inde...) while((s32[]{:T(128)}, f32[384,256]{1,0:T(8,128)S(1)}, ...), condition=%wide.region_38.39_spmd.clone, body=%wide.region_36.38_spmd.clone.sunk | while | flops 508100096 | bytes 9079975 | solution.py:107
  559.1 1.0 fusion.262
  562.0 1.0 fusion.262
  564.8 1.0 fusion.262
  567.6 1.0 fusion.262
  570.4 1.0 fusion.262
  573.2 1.0 fusion.262
  576.8 343.0 %all-reduce.2 = (f32[]{:T(128)}, f32[]{:T(128)}) all-reduce(f32[]{:T(128)} %get-tuple-element.718, f32[]{:T(128)} %get-tuple-element.717), channel_id=1, replica_groups=mesh['filt'=2,'row'=4,'col'=32] {'row','col'}, use_global_device_ids=true, to_apply=%region_44.45 | all-reduce | flops 2 | bytes 16 | tf_op jit(solution)/shard_map/psum | solution.py:120
  922.5 1.5 add_convert_fusion
  (327 shorter events, 65.9 us)
Async XLA Ops:
  7.2 116.7 %all-gather.6.cloned.1.call-start = ((), (), s32[]{:S(2)}) async-start(), calls=%async_computation.1 | async-start | bytes 1622016 | tf_op jit(solution)/shard_map/all_gather | solution.py:12
  7.9 914.6 %reduce-scatter.2.cloned.1.call-start = ((), (), s32[]{:S(2)}) async-start(), calls=%async_computation.3 | async-start | bytes 245760 | tf_op jit(solution)/shard_map/reduce_scatter | solution.py:114
  123.8 2.1 copy-start
  340.3 0.6 copy-start.1
  416.0 0.6 copy-start.2
  484.3 0.6 copy-start.3
  574.7 1.5 copy-start.4
  575.4 347.1 %all-reduce.7.cloned.1.call-start = ((), (), s32[]{:S(2)}) async-start(), calls=%async_computation.2 | async-start | bytes 3145728 | tf_op jit(solution)/shard_map/psum | solution.py:112
Sparse Core Ops, SparseCore 0:
  10.6 78.8 all-gather.5
  575.5 17.6 reduce-scatter.1
  597.0 150.1 all-reduce.6
